TPU v7x, 256 devices: a whole 4x4x8 slice. The times are simulated.
256 devices in a mesh: seq: 32 (over z, y), tp: 8 (over x, core).
Axes of the slice: x: 4, y: 4, z: 8, core: 2. Of those that a mesh axis runs over, the one named last changes fastest.
Arguments:
- tokens: bfloat16 [16384, 4096], P('seq'), may hold values from -80 to 80
- norm_gain: float32 [4096], replicated, may hold values from 0.1 to 1.9
- query_weight: bfloat16 [4096, 4096], P(None, 'tp'), may hold values from -1 to 1
- key_weight: bfloat16 [4096, 1024], P(None, 'tp'), may hold values from -8 to 8
- value_weight: bfloat16 [4096, 1024], P(None, 'tp'), may hold values from -0.09375 to 0.09375
- out_weight: bfloat16 [4096, 4096], P(None, 'tp'), may hold values from -1 to 1
- segments: int32 [16384], replicated, may hold values from 0 to 2, never falling along the last dimension, each value on 1 to 8192 neighbouring positions
Outputs:
- attn_out: bfloat16 [16384, 4096], P('seq', 'tp')
All inputs are finite; a program needn't handle non-finite values.
Results may differ from a plain program's by a relative error of at most 0.013.
The roundings to bfloat16 on the way count: a program that leaves them out, or rounds other values in their place, can miss the bound.
Values may be sent and summed in bfloat16 or wider, within the bound.
A program may use at most 128 MiB of HBM per device.

v0:
```python
import math
import jax
import jax.numpy as jnp
from jax import lax
from jax.sharding import PartitionSpec as P

HEAD_DIM = 128
WINDOW = 4096


def shifted(value, axis, steps):
    count = lax.axis_size(axis)
    leading, last = (max(0, -steps), min(count, count - steps))
    return lax.ppermute(value, axis, [(source, source + steps) for source in range(leading, last)])


def rotate(vectors, positions):
    half_dim = vectors.shape[-1] // 2
    freqs = 10000.0 ** (-(jnp.arange(half_dim, dtype=jnp.float32) * 2.0 / vectors.shape[-1]))
    angles = positions[:, None] * freqs[None, :]
    cosine = jnp.cos(angles)[:, None, :]
    sine_part = jnp.sin(angles)[:, None, :]
    first = vectors[..., :half_dim]
    second = vectors[..., half_dim:]
    return jnp.concatenate(
        [first * cosine - second * sine_part, second * cosine + first * sine_part], axis=-1
    )


def project(normed, weight, positions):
    product = jnp.dot(normed, weight, preferred_element_type=jnp.float32)
    shaped = product.reshape(product.shape[0], -1, HEAD_DIM)
    return rotate(shaped, positions).astype(jnp.bfloat16)


def attend(queries, keys, values, allowed):
    block_rows, query_heads, head_size = queries.shape
    value_heads = keys.shape[1]
    grouped = queries.reshape(block_rows, value_heads, query_heads // value_heads, head_size)
    scores = jnp.einsum(
        "tkgd,skd->kgts", grouped, keys, preferred_element_type=jnp.float32
    ) / math.sqrt(head_size)
    scores = jnp.where(allowed[None, None], scores, jnp.float32(-1e30))
    peak = jnp.max(scores, axis=-1, keepdims=True)
    weights = jnp.exp(scores - peak)
    totals = jnp.sum(weights, axis=-1, keepdims=True)
    probabilities = (weights / totals).astype(jnp.bfloat16)
    attended = jnp.einsum(
        "kgts,skd->tkgd", probabilities, values, preferred_element_type=jnp.float32
    )
    return attended.reshape(block_rows, query_heads * head_size).astype(jnp.bfloat16)


def shards(tokens, norm_gain, query_weight, key_weight, value_weight, out_weight, segments):
    block_rows = tokens.shape[0]
    seq_index = lax.axis_index("seq")
    seq_count = lax.axis_size("seq")
    halo_blocks = min((WINDOW + block_rows - 2) // block_rows, seq_count - 1)
    widened = tokens.astype(jnp.float32)
    scale = lax.rsqrt(jnp.mean(widened * widened, axis=-1, keepdims=True) + 1e-05)
    normed = (widened * scale * norm_gain[None, :]).astype(jnp.bfloat16)
    first_token = seq_index * block_rows
    positions = (first_token + jnp.arange(block_rows, dtype=jnp.int32)).astype(jnp.float32)
    queries = project(normed, query_weight, positions)
    keys = project(normed, key_weight, positions)
    value_heads = keys.shape[1]
    values = jnp.dot(normed, value_weight, preferred_element_type=jnp.float32).astype(jnp.bfloat16)
    key_width = value_heads * HEAD_DIM
    key_value = jnp.concatenate([keys.reshape(block_rows, key_width), values], axis=1)
    front = halo_blocks * block_rows
    known_blocks = key_value
    gathered_count = 0
    while gathered_count < halo_blocks:
        taking = min(gathered_count + 1, halo_blocks - gathered_count)
        outgoing = known_blocks[known_blocks.shape[0] - taking * block_rows :]
        incoming = shifted(outgoing, "seq", gathered_count + 1)
        known_blocks = jnp.concatenate([incoming, known_blocks], axis=0)
        gathered_count = gathered_count + taking
    before = known_blocks[:front]
    window_rows = jnp.concatenate([before, key_value], axis=0)
    span = window_rows.shape[0]
    window_keys = window_rows[:, :key_width].reshape(span, value_heads, HEAD_DIM)
    window_values = window_rows[:, key_width:].reshape(span, value_heads, HEAD_DIM)
    padded_segments = jnp.concatenate([jnp.full((front,), -1, jnp.int32), segments], axis=0)
    start_index = seq_index * block_rows
    key_segments = lax.dynamic_slice_in_dim(padded_segments, start_index, span, 0)
    query_segments = lax.dynamic_slice_in_dim(segments, start_index, block_rows, 0)
    query_pos = start_index + jnp.arange(block_rows, dtype=jnp.int32)
    key_pos = start_index - front + jnp.arange(span, dtype=jnp.int32)
    distance = query_pos[:, None] - key_pos[None, :]
    allowed = (
        (distance >= 0) & (distance < WINDOW) & (key_segments[None, :] == query_segments[:, None])
    )
    attended = attend(queries, window_keys, window_values, allowed)
    projected = jnp.dot(
        lax.all_gather(attended, "tp", axis=1, tiled=True),
        out_weight,
        preferred_element_type=jnp.float32,
    )
    return projected.astype(jnp.bfloat16)


def solution(mesh):
    return jax.shard_map(
        shards,
        mesh=mesh,
        in_specs=(
            P("seq", None),
            P(),
            P(None, "tp"),
            P(None, "tp"),
            P(None, "tp"),
            P(None, "tp"),
            P(),
        ),
        out_specs=P("seq", "tp"),
        check_vma=False,
    )
```

profile of v0, /device:TPU:1, one launch (start us, length us, event | category | flops | bytes accessed | tf_op | source)
XLA Modules:
  0.0 180.7 jit_solution(8147630564713881535)
XLA Ops:
  6.5 0.0 copy-start
  6.5 0.0 all-gather.2.cloned.1.call-start
  6.6 0.0 copy-start.2
  6.6 3.2 %fusion.6 = f32[512]{0:T(512)S(1)} fusion(bf16[512,4096]{1,0:T(8,128)(2,1)} %param.7), kind=kLoop, calls=%fused_computation.13 | loop fusion | flops 6290944 | bytes 4196352 | tf_op jit(solution)/shard_map/reduce_sum | solution.py:60
  9.8 0.5 copy-done.2
  10.3 1.6 convolution_convert_fusion.1
  12.0 0.0 copy-start.12
  12.0 1.6 convolution_bitcast_fusion
  13.6 0.0 copy-start.16
  13.6 0.6 fusion.25
  14.2 0.7 pad_maximum_fusion
  14.9 4.0 %collective-permute-start.1 = (bf16[512,256]{0,1:T(8,128)(2,1)}, bf16[512,256]{0,1:T(8,128)(2,1)S(1)}, u32[]{:S(2)}, u32[]{:S(2)}) collective-permute-start(bf16[512,256]{0,1:T(8,128)(2,1)} %pad_maximum_fusion), channel_id=1, source_target_pairs={{0,8},{8,16},{16,24},{24,32},{32,40},{40,48},{48,56},{56,64},{64,7... | collective-permute-start | bytes 786440 | tf_op jit(solution)/shard_map/ppermute | solution.py:14
  18.9 5.6 %collective-permute-start = (bf16[512,256]{0,1:T(8,128)(2,1)}, bf16[512,256]{0,1:T(8,128)(2,1)}, u32[]{:S(2)}, u32[]{:S(2)}) collective-permute-start(bf16[512,256]{0,1:T(8,128)(2,1)} %pad_maximum_fusion), channel_id=1, source_target_pairs={{0,64},{8,72},{16,80},{24,88},{32,96},{40,104},{48,112},{56,120},{... | collective-permute-start | bytes 786440 | tf_op jit(solution)/shard_map/ppermute | solution.py:14
  24.5 0.1 dynamic_slice.7
  24.6 0.1 pad_dynamic-slice_fusion
  24.7 0.0 collective-permute-done.1
  24.7 0.1 maximum_maximum_fusion.1
  24.8 5.3 %collective-permute-start.2 = (bf16[1024,256]{0,1:T(8,128)(2,1)S(1)}, bf16[1024,256]{0,1:T(8,128)(2,1)S(1)}, u32[]{:S(2)}, u32[]{:S(2)}) collective-permute-start(bf16[1024,256]{0,1:T(8,128)(2,1)S(1)} %maximum_maximum_fusion.1), channel_id=1, source_target_pairs={{0,16},{8,24},{16,32},{24,40},{32,48},{40,56},{48,64},{56,72},{64,... | collective-permute-start | bytes 1572872 | tf_op jit(solution)/shard_map/ppermute | solution.py:14
  30.1 3.8 %fusion.5 = pred[512,4608]{0,1:T(8,128)(4,1)S(1)} fusion(s32[512]{0:T(512)S(1)} %dynamic_slice.7, s32[4608]{0:T(1024)S(1)} %get-tuple-element.16, s32[512]{0:T(512)S(1)} %iota_add_fusion.1, s32[4608]{0:T(1024)S(1)} %get-tuple-element.15), kind=kLoop, calls=%fused_computation.12 | loop fusion | flops 14155776 | bytes 2400256 | tf_op jit(solution)/shard_map/and | solution.py:92
  33.8 5.9 %collective-permute-done.2 = bf16[1024,256]{0,1:T(8,128)(2,1)S(1)} collective-permute-done((bf16[1024,256]{0,1:T(8,128)(2,1)S(1)}, bf16[1024,256]{0,1:T(8,128)(2,1)S(1)}, u32[]{:S(2)}, u32[]{:S(2)}) %collective-permute-start.2) | collective-permute-done | bytes 524320 | tf_op jit(solution)/shard_map/ppermute | solution.py:14
  39.7 1.1 maximum_maximum_fusion
  40.9 7.5 %collective-permute-start.3 = (bf16[2048,256]{0,1:T(8,128)(2,1)}, bf16[2048,256]{0,1:T(8,128)(2,1)}, u32[]{:S(2)}, u32[]{:S(2)}) collective-permute-start(bf16[2048,256]{0,1:T(8,128)(2,1)} %maximum_maximum_fusion), channel_id=1, source_target_pairs={{0,32},{8,40},{16,48},{24,56},{32,64},{40,72},{48,80},{56,88},{64,... | collective-permute-start | bytes 3145736 | tf_op jit(solution)/shard_map/ppermute | solution.py:14
  48.4 0.0 copy-done.16
  48.4 4.8 %fusion.30 = f32[512,512]{0,1:T(8,128)S(1)} fusion(bf16[4096,512]{1,0:T(8,128)(2,1)} %param.9, bf16[512,4096]{1,0:T(8,128)(2,1)S(1)} %copy-done.3, f32[4096]{0:T(1024)S(1)} %copy-done.16, f32[512]{0:T(512)S(1)} %add_rsqrt_fusion), kind=kOutput, calls=%fused_computation.59 | convolution fusion | flops 2155872256 | bytes 9455616 | tf_op jit(solution)/shard_map/dot_general | solution.py:31
  53.2 0.0 copy-done.8
  53.2 0.0 copy-done.10
  53.2 0.0 copy-done.4
  53.2 0.0 copy-done.6
  53.2 1.1 fusion.34
  54.3 1.4 copy.16
  55.6 2.4 %copy.15 = f32[512,4,64]{2,0,1:T(8,128)} copy(f32[512,4,64]{0,2,1:T(8,128)} %get-tuple-element.8) | data formatting | bytes 1048576
  58.0 1.0 multiply_cosine_fusion
  59.0 1.5 subtract_convert_fusion
  60.5 0.0 collective-permute-done
  60.6 1.0 constant_dynamic-update-slice_fusion.4
  61.5 5.6 %collective-permute-done.3 = bf16[2048,256]{0,1:T(8,128)(2,1)} collective-permute-done((bf16[2048,256]{0,1:T(8,128)(2,1)}, bf16[2048,256]{0,1:T(8,128)(2,1)}, u32[]{:S(2)}, u32[]{:S(2)}) %collective-permute-start.3) | collective-permute-done | bytes 1048608 | tf_op jit(solution)/shard_map/ppermute | solution.py:14
  67.1 1.3 constant_dynamic-update-slice_fusion.3
  68.5 0.0 copy-done.7
  68.5 0.0 copy-done.9
  68.6 0.0 copy-done.11
  68.6 15.3 %fusion.1 = (f32[4,512]{1,0:T(4,128)S(1)}, f32[4608,512,4]{1,0,2:T(8,128)}) fusion(pred[512,4608]{0,1:T(8,128)(4,1)S(1)} %fusion.5, bf16[512,4,64]{2,0,1:T(8,128)(2,1)S(1)} %get-tuple-element.6, bf16[512,4,64]{2,0,1:T(8,128)(2,1)S(1)} %get-tuple-element.5, bf16[4608,256]{0,1:T(8,128)(2,1)S(1)} %constant_dynamic-update-slice_fusion), kind=kOutput, calls=%fused_computation.4 | convolution fusion | flops 2445277184 | bytes 42344448 | tf_op jit(solution)/shard_map/tkgd,skd->kgts/dot_general | solution.py:40
  83.9 0.0 copy-done.13
  83.9 16.0 %fusion = f32[4,512]{1,0:T(4,128)S(1)} fusion(f32[4608,512,4]{1,0,2:T(8,128)} %get-tuple-element.14, f32[4,512]{1,0:T(4,128)S(1)} %get-tuple-element.13, pred[512,4608]{0,1:T(8,128)(4,1)S(1)} %fusion.5), kind=kLoop, calls=%fused_computation.3 | loop fusion | flops 37746688 | bytes 40124416 | tf_op jit(solution)/shard_map/reduce_sum | solution.py:46
  99.9 18.3 %fusion.9 = bf16[128,4,512]{2,0,1:T(8,128)(2,1)} fusion(f32[4,512]{1,0:T(4,128)S(1)} %fusion, f32[4,512]{1,0:T(4,128)S(1)} %get-tuple-element.13, f32[4608,512,4]{1,0,2:T(8,128)} %get-tuple-element.14, pred[512,4608]{0,1:T(8,128)(4,1)S(1)} %fusion.5, bf16[4608,256]{0,1:T(8,128)(2,1)} %copy-done.13), kind=kOutput, calls=%fused_computation.17 | convolution fusion | flops 2463367168 | bytes 41828352 | tf_op jit(solution)/shard_map/kgts,skd->tkgd/dot_general | solution.py:48
  118.2 0.0 all-gather.2.cloned.1.call-update
  118.3 0.0 copy-start.1
  118.3 48.9 %all-gather.2.cloned.1.call-done = bf16[512,4096]{0,1:T(8,128)(2,1)} async-done(((bf16[512,512]{0,1:T(8,128)(2,1)}), bf16[512,4096]{0,1:T(8,128)(2,1)}) %all-gather.2.cloned.1.call-update) | async-done | bytes 4194320 | tf_op jit(solution)/shard_map/all_gather | solution.py:96
  167.2 6.6 %convolution_convert_fusion = bf16[512,512]{1,0:T(8,128)(2,1)} fusion(bf16[512,4096]{0,1:T(8,128)(2,1)} %all-gather.2.cloned.1.call-done, bf16[4096,512]{1,0:T(8,128)(2,1)} %param.12), kind=kOutput, calls=%fused_computation.16 | convolution fusion | flops 2147745792 | bytes 8912896 | tf_op jit(solution)/shard_map/dot_general | solution.py:95
  (26 shorter events, 0.1 us)
Async XLA Ops:
  6.5 3.3 %copy-start = (bf16[4096,128]{1,0:T(8,128)(2,1)S(1)}, bf16[4096,128]{1,0:T(8,128)(2,1)}, u32[]{:S(2)}) copy-start(bf16[4096,128]{1,0:T(8,128)(2,1)} %param.11) | copy-start | bytes 3145732
  6.5 3.3 %copy-start.15 = (f32[4096]{0:T(1024)S(1)}, f32[4096]{0:T(1024)}, u32[]{:S(2)}) copy-start(f32[4096]{0:T(1024)} %param.8) | copy-start | bytes 49156
  6.5 160.7 %all-gather.2.cloned.1.call-start = ((), (), s32[]{:S(2)}) async-start(), calls=%async_computation | async-start | bytes 4718592 | tf_op jit(solution)/shard_map/all_gather | solution.py:96
  6.6 3.8 %copy-start.2 = (bf16[512,4096]{1,0:T(8,128)(2,1)S(1)}, bf16[512,4096]{1,0:T(8,128)(2,1)}, u32[]{:S(2)}) copy-start(bf16[512,4096]{1,0:T(8,128)(2,1)} %param.7) | copy-start | bytes 12582916
  10.3 1.6 copy-start.14
  12.0 12.6 %copy-start.12 = (s32[16384]{0:T(1024)S(1)}, s32[16384]{0:T(1024)}, u32[]{:S(2)}) copy-start(s32[16384]{0:T(1024)} %param.13) | copy-start | bytes 196612
  13.6 34.8 %copy-start.16 = (f32[4096]{0:T(1024)S(1)}, f32[4096]{0:T(1024)}, u32[]{:S(2)}) copy-start(f32[4096]{0:T(1024)} %param.8) | copy-start | bytes 49156
  14.2 39.0 %copy-start.8 = (bf16[512,64]{0,1:T(8,128)(2,1)}, bf16[512,64]{0,1:T(8,128)(2,1)S(1)}, u32[]{:S(2)}) copy-start(bf16[512,64]{0,1:T(8,128)(2,1)S(1)} %get-tuple-element.9) | copy-start | bytes 196612
  14.2 39.0 %copy-start.10 = (bf16[512,64]{0,1:T(8,128)(2,1)}, bf16[512,64]{0,1:T(8,128)(2,1)S(1)}, u32[]{:S(2)}) copy-start(bf16[512,64]{0,1:T(8,128)(2,1)S(1)} %get-tuple-element.10) | copy-start | bytes 196612
  14.9 9.8 %collective-permute-start.1 = (bf16[512,256]{0,1:T(8,128)(2,1)}, bf16[512,256]{0,1:T(8,128)(2,1)S(1)}, u32[]{:S(2)}, u32[]{:S(2)}) collective-permute-start(bf16[512,256]{0,1:T(8,128)(2,1)} %pad_maximum_fusion), channel_id=1, source_target_pairs={{0,8},{8,16},{16,24},{24,32},{32,40},{40,48},{48,56},{56,64},{64,7... | collective-permute-start | bytes 786440 | tf_op jit(solution)/shard_map/ppermute | solution.py:14
  18.9 41.6 %collective-permute-start = (bf16[512,256]{0,1:T(8,128)(2,1)}, bf16[512,256]{0,1:T(8,128)(2,1)}, u32[]{:S(2)}, u32[]{:S(2)}) collective-permute-start(bf16[512,256]{0,1:T(8,128)(2,1)} %pad_maximum_fusion), channel_id=1, source_target_pairs={{0,64},{8,72},{16,80},{24,88},{32,96},{40,104},{48,112},{56,120},{... | collective-permute-start | bytes 786440 | tf_op jit(solution)/shard_map/ppermute | solution.py:14
  24.5 23.9 %copy-start.3 = (bf16[512,4096]{1,0:T(8,128)(2,1)S(1)}, bf16[512,4096]{1,0:T(8,128)(2,1)}, u32[]{:S(2)}) copy-start(bf16[512,4096]{1,0:T(8,128)(2,1)} %param.7) | copy-start | bytes 12582916
  24.7 28.5 %copy-start.4 = (bf16[512,256]{0,1:T(8,128)(2,1)}, bf16[512,256]{0,1:T(8,128)(2,1)S(1)}, u32[]{:S(2)}) copy-start(bf16[512,256]{0,1:T(8,128)(2,1)S(1)} %collective-permute-done.1) | copy-start | bytes 786436
  24.8 15.0 %collective-permute-start.2 = (bf16[1024,256]{0,1:T(8,128)(2,1)S(1)}, bf16[1024,256]{0,1:T(8,128)(2,1)S(1)}, u32[]{:S(2)}, u32[]{:S(2)}) collective-permute-start(bf16[1024,256]{0,1:T(8,128)(2,1)S(1)} %maximum_maximum_fusion.1), channel_id=1, source_target_pairs={{0,16},{8,24},{16,32},{24,40},{32,48},{40,56},{48,64},{56,72},{64,... | collective-permute-start | bytes 1572872 | tf_op jit(solution)/shard_map/ppermute | solution.py:14
  39.7 13.5 %copy-start.6 = (bf16[1024,256]{0,1:T(8,128)(2,1)}, bf16[1024,256]{0,1:T(8,128)(2,1)S(1)}, u32[]{:S(2)}) copy-start(bf16[1024,256]{0,1:T(8,128)(2,1)S(1)} %collective-permute-done.2) | copy-start | bytes 1572868
  40.9 26.3 %collective-permute-start.3 = (bf16[2048,256]{0,1:T(8,128)(2,1)}, bf16[2048,256]{0,1:T(8,128)(2,1)}, u32[]{:S(2)}, u32[]{:S(2)}) collective-permute-start(bf16[2048,256]{0,1:T(8,128)(2,1)} %maximum_maximum_fusion), channel_id=1, source_target_pairs={{0,32},{8,40},{16,48},{24,56},{32,64},{40,72},{48,80},{56,88},{64,... | collective-permute-start | bytes 3145736 | tf_op jit(solution)/shard_map/ppermute | solution.py:14
  58.0 10.4 %copy-start.7 = (bf16[1024,256]{0,1:T(8,128)(2,1)S(1)}, bf16[1024,256]{0,1:T(8,128)(2,1)}, u32[]{:S(2)}) copy-start(bf16[1024,256]{0,1:T(8,128)(2,1)} %copy-done.6) | copy-start | bytes 1572868
  58.0 10.5 %copy-start.5 = (bf16[512,256]{0,1:T(8,128)(2,1)S(1)}, bf16[512,256]{0,1:T(8,128)(2,1)}, u32[]{:S(2)}) copy-start(bf16[512,256]{0,1:T(8,128)(2,1)} %copy-done.4) | copy-start | bytes 786436
  58.0 10.5 %copy-start.9 = (bf16[512,64]{0,1:T(8,128)(2,1)S(1)}, bf16[512,64]{0,1:T(8,128)(2,1)}, u32[]{:S(2)}) copy-start(bf16[512,64]{0,1:T(8,128)(2,1)} %copy-done.8) | copy-start | bytes 196612
  58.0 10.5 %copy-start.11 = (bf16[512,64]{0,1:T(8,128)(2,1)S(1)}, bf16[512,64]{0,1:T(8,128)(2,1)}, u32[]{:S(2)}) copy-start(bf16[512,64]{0,1:T(8,128)(2,1)} %copy-done.10) | copy-start | bytes 196612
  68.6 15.3 %copy-start.13 = (bf16[4608,256]{0,1:T(8,128)(2,1)}, bf16[4608,256]{0,1:T(8,128)(2,1)S(1)}, u32[]{:S(2)}) copy-start(bf16[4608,256]{0,1:T(8,128)(2,1)S(1)} %constant_dynamic-update-slice_fusion) | copy-start | bytes 7077892
  118.3 55.5 %copy-start.1 = (bf16[4096,128]{1,0:T(8,128)(2,1)S(1)}, bf16[4096,128]{1,0:T(8,128)(2,1)}, u32[]{:S(2)}) copy-start(bf16[4096,128]{1,0:T(8,128)(2,1)} %param.11) | copy-start | bytes 3145732
Sparse Core Ops, SparseCore 0:
  118.4 48.7 all-gather.1
where the time goes:
time: 181 us
  waiting for transfers between devices  60.5 us (33%)
  matrix products  48.2 us (27%)
  other arithmetic  28.1 us (16%)
  starting transfers between devices  22.4 us (12%)
  between operations  13.7 us (8%)
  local copies, waits for them, and re-layouts  7.74 us (4%)
    all_gather x1, waiting for transfers between devices, shards(): lax.all_gather(attended, 'tp', axis=1, tiled=True)  48.9 us
    ppermute x4, starting transfers between devices, shifted(): lax.ppermute(value, axis, [(source, source + steps) for source in range(l...  22.4 us
    dot_general x1, matrix products, attend(): jnp.einsum('kgts,skd->tkgd', probabilities, values, preferred_element_typ...  18.3 us
    reduce_sum x1, other arithmetic, attend(): totals = jnp.sum(weights, axis=-1, keepdims=True)  16 us
    dot_general x1, matrix products, attend(): jnp.einsum('tkgd,skd->kgts', grouped, keys, preferred_element_type=jnp.fl...  15.3 us
    ppermute x4, waiting for transfers between devices, shifted(): lax.ppermute(value, axis, [(source, source + steps) for source in range(l...  11.6 us
    unnamed x40, local copies, waits for them, and re-layouts  6.61 us
    dot_general x1, matrix products, shards(): jnp.dot(lax.all_gather(attended, 'tp', axis=1, tiled=True), out_weight, p...  6.61 us
  transfers between devices with their start and end apart: 5, of which 3 were waited for; matrix products, arithmetic and copies ran while one was open for 10% of the time, Pallas kernels for 0%

commit v1 on v0

--- a/solution.py
+++ b/solution.py
@@ -6,6 +6,12 @@
 
 HEAD_DIM = 128
 WINDOW = 4096
+
+
+def save_node_by_axis(patch, axis_tag):
+    return jax.lax.all_to_all(
+        jnp.concatenate([patch] * jax.lax.axis_size(axis_tag), axis=1), axis_tag, 1, 1, tiled=True
+    )
 
 
 def shifted(value, axis, steps):
@@ -93,9 +99,7 @@
     )
     attended = attend(queries, window_keys, window_values, allowed)
     projected = jnp.dot(
-        lax.all_gather(attended, "tp", axis=1, tiled=True),
-        out_weight,
-        preferred_element_type=jnp.float32,
+        save_node_by_axis(attended, "tp"), out_weight, preferred_element_type=jnp.float32
     )
     return projected.astype(jnp.bfloat16)
 

time: 181 us -> 191 us (1.055)
  the two profiles are of different devices: /device:TPU:1 before, /device:TPU:136 now
where the time goes in v1:
time: 191 us; the launch traced here: 190 us
  blocking collectives  53.9 us (28%)
  matrix products  47.7 us (25%)
  waiting for transfers between devices  32.5 us (17%)
  other arithmetic  28.2 us (15%)
  local copies, waits for them, and re-layouts  14.9 us (8%)
  starting transfers between devices  13 us (7%)
    all_to_all x1, blocking collectives, save_node_by_axis(): jax.lax.all_to_all(jnp.concatenate([patch] * jax.lax.axis_size(axis_tag),...  53.9 us
    ppermute x4, waiting for transfers between devices, shifted(): lax.ppermute(value, axis, [(source, source + steps) for source in range(l...  32.5 us
    dot_general x1, matrix products, attend(): jnp.einsum('kgts,skd->tkgd', probabilities, values, preferred_element_typ...  17.6 us
    reduce_sum x1, other arithmetic, attend(): totals = jnp.sum(weights, axis=-1, keepdims=True)  16 us
    dot_general x1, matrix products, attend(): jnp.einsum('tkgd,skd->kgts', grouped, keys, preferred_element_type=jnp.fl...  15.3 us
    ppermute x4, starting transfers between devices, shifted(): lax.ppermute(value, axis, [(source, source + steps) for source in range(l...  13 us
    dot_general x1, matrix products, shards(): jnp.dot(save_node_by_axis(attended, 'tp'), out_weight, preferred_element_...  6.68 us
    unnamed x40, local copies, waits for them, and re-layouts  6.61 us
  transfers between devices with their start and end apart: 4, of which 3 were waited for; matrix products, arithmetic and copies ran while one was open for 10% of the time, Pallas kernels for 0%

profile of v1, /device:TPU:136, one launch (start us, length us, event | category | flops | bytes accessed | tf_op | source)
XLA Modules:
  0.0 190.5 jit_solution(8420284735642032241)
XLA Ops:
  0.0 0.0 copy-start
  0.0 0.0 copy-start.2
  0.0 3.2 %fusion.6 = f32[512]{0:T(512)S(1)} fusion(bf16[512,4096]{1,0:T(8,128)(2,1)} %param.7), kind=kLoop, calls=%fused_computation.13 | loop fusion | flops 6290944 | bytes 4196352 | tf_op jit(solution)/shard_map/reduce_sum | solution.py:66
  3.3 0.0 copy-done
  3.3 0.0 copy-done.15
  3.3 0.5 copy-done.2
  3.8 1.6 convolution_convert_fusion.1
  5.4 0.0 copy-done.14
  5.4 0.0 copy-start.12
  5.4 1.6 convolution_bitcast_fusion
  7.0 0.0 copy-start.16
  7.1 0.6 fusion.25
  7.6 0.0 copy-start.8
  7.6 0.0 copy-start.10
  7.6 0.7 pad_maximum_fusion
  8.4 3.5 %collective-permute-start.1 = (bf16[512,256]{0,1:T(8,128)(2,1)}, bf16[512,256]{0,1:T(8,128)(2,1)S(1)}, u32[]{:S(2)}, u32[]{:S(2)}) collective-permute-start(bf16[512,256]{0,1:T(8,128)(2,1)} %pad_maximum_fusion), channel_id=1, source_target_pairs={{0,8},{8,16},{16,24},{24,32},{32,40},{40,48},{48,56},{56,64},{64,7... | collective-permute-start | bytes 786440 | tf_op jit(solution)/shard_map/ppermute | solution.py:20
  11.9 3.4 %collective-permute-start = (bf16[512,256]{0,1:T(8,128)(2,1)}, bf16[512,256]{0,1:T(8,128)(2,1)}, u32[]{:S(2)}, u32[]{:S(2)}) collective-permute-start(bf16[512,256]{0,1:T(8,128)(2,1)} %pad_maximum_fusion), channel_id=1, source_target_pairs={{0,64},{8,72},{16,80},{24,88},{32,96},{40,104},{48,112},{56,120},{... | collective-permute-start | bytes 786440 | tf_op jit(solution)/shard_map/ppermute | solution.py:20
  15.2 0.0 copy-done.12
  15.3 0.0 copy-start.3
  15.3 0.1 dynamic_slice.7
  15.3 0.1 pad_dynamic-slice_fusion
  15.4 3.1 %collective-permute-done.1 = bf16[512,256]{0,1:T(8,128)(2,1)S(1)} collective-permute-done((bf16[512,256]{0,1:T(8,128)(2,1)}, bf16[512,256]{0,1:T(8,128)(2,1)S(1)}, u32[]{:S(2)}, u32[]{:S(2)}) %collective-permute-start.1) | collective-permute-done | bytes 262176 | tf_op jit(solution)/shard_map/ppermute | solution.py:20
  18.5 0.1 maximum_maximum_fusion.1
  18.6 4.2 %collective-permute-start.2 = (bf16[1024,256]{0,1:T(8,128)(2,1)S(1)}, bf16[1024,256]{0,1:T(8,128)(2,1)S(1)}, u32[]{:S(2)}, u32[]{:S(2)}) collective-permute-start(bf16[1024,256]{0,1:T(8,128)(2,1)S(1)} %maximum_maximum_fusion.1), channel_id=1, source_target_pairs={{0,16},{8,24},{16,32},{24,40},{32,48},{40,56},{48,64},{56,72},{64,... | collective-permute-start | bytes 1572872 | tf_op jit(solution)/shard_map/ppermute | solution.py:20
  22.8 3.8 %fusion.5 = pred[512,4608]{0,1:T(8,128)(4,1)S(1)} fusion(s32[512]{0:T(512)S(1)} %dynamic_slice.7, s32[4608]{0:T(1024)S(1)} %get-tuple-element.16, s32[512]{0:T(512)S(1)} %iota_add_fusion.1, s32[4608]{0:T(1024)S(1)} %get-tuple-element.15), kind=kLoop, calls=%fused_computation.12 | loop fusion | flops 14155776 | bytes 2400256 | tf_op jit(solution)/shard_map/and | solution.py:98
  26.5 17.1 %collective-permute-done.2 = bf16[1024,256]{0,1:T(8,128)(2,1)S(1)} collective-permute-done((bf16[1024,256]{0,1:T(8,128)(2,1)S(1)}, bf16[1024,256]{0,1:T(8,128)(2,1)S(1)}, u32[]{:S(2)}, u32[]{:S(2)}) %collective-permute-start.2) | collective-permute-done | bytes 524320 | tf_op jit(solution)/shard_map/ppermute | solution.py:20
  43.6 1.2 maximum_maximum_fusion
  44.8 1.9 %collective-permute-start.3 = (bf16[2048,256]{0,1:T(8,128)(2,1)}, bf16[2048,256]{0,1:T(8,128)(2,1)}, u32[]{:S(2)}, u32[]{:S(2)}) collective-permute-start(bf16[2048,256]{0,1:T(8,128)(2,1)} %maximum_maximum_fusion), channel_id=1, source_target_pairs={{0,32},{8,40},{16,48},{24,56},{32,64},{40,72},{48,80},{56,88},{64,... | collective-permute-start | bytes 3145736 | tf_op jit(solution)/shard_map/ppermute | solution.py:20
  46.7 0.0 copy-done.16
  46.7 0.0 copy-done.3
  46.7 4.8 %fusion.30 = f32[512,512]{0,1:T(8,128)S(1)} fusion(bf16[4096,512]{1,0:T(8,128)(2,1)} %param.9, bf16[512,4096]{1,0:T(8,128)(2,1)S(1)} %copy-done.3, f32[4096]{0:T(1024)S(1)} %copy-done.16, f32[512]{0:T(512)S(1)} %add_rsqrt_fusion), kind=kOutput, calls=%fused_computation.59 | convolution fusion | flops 2155872256 | bytes 9455616 | tf_op jit(solution)/shard_map/dot_general | solution.py:37
  51.6 1.1 fusion.34
  52.6 1.4 copy.28
  54.0 2.4 %copy.27 = f32[512,4,64]{2,0,1:T(8,128)} copy(f32[512,4,64]{0,2,1:T(8,128)} %get-tuple-element.8) | data formatting | bytes 1048576
  56.4 1.0 multiply_cosine_fusion
  57.4 1.5 subtract_convert_fusion
  58.9 0.0 collective-permute-done
  58.9 1.0 constant_dynamic-update-slice_fusion.4
  59.9 12.4 %collective-permute-done.3 = bf16[2048,256]{0,1:T(8,128)(2,1)} collective-permute-done((bf16[2048,256]{0,1:T(8,128)(2,1)}, bf16[2048,256]{0,1:T(8,128)(2,1)}, u32[]{:S(2)}, u32[]{:S(2)}) %collective-permute-start.3) | collective-permute-done | bytes 1048608 | tf_op jit(solution)/shard_map/ppermute | solution.py:20
  72.3 1.3 constant_dynamic-update-slice_fusion.3
  73.7 15.3 %fusion.1 = (f32[4,512]{1,0:T(4,128)S(1)}, f32[4608,512,4]{1,0,2:T(8,128)}) fusion(pred[512,4608]{0,1:T(8,128)(4,1)S(1)} %fusion.5, bf16[512,4,64]{2,0,1:T(8,128)(2,1)S(1)} %get-tuple-element.6, bf16[512,4,64]{2,0,1:T(8,128)(2,1)S(1)} %get-tuple-element.5, bf16[4608,256]{0,1:T(8,128)(2,1)S(1)} %constant_dynamic-update-slice_fusion), kind=kOutput, calls=%fused_computation.4 | convolution fusion | flops 2445277184 | bytes 42344448 | tf_op jit(solution)/shard_map/tkgd,skd->kgts/dot_general | solution.py:46
  89.1 16.0 %fusion = f32[4,512]{1,0:T(4,128)S(1)} fusion(f32[4608,512,4]{1,0,2:T(8,128)} %get-tuple-element.14, f32[4,512]{1,0:T(4,128)S(1)} %get-tuple-element.13, pred[512,4608]{0,1:T(8,128)(4,1)S(1)} %fusion.5), kind=kLoop, calls=%fused_computation.3 | loop fusion | flops 37746688 | bytes 40124416 | tf_op jit(solution)/shard_map/reduce_sum | solution.py:52
  105.1 17.6 %fusion.9 = bf16[128,4,512]{2,0,1:T(8,128)(2,1)S(1)} fusion(f32[4,512]{1,0:T(4,128)S(1)} %fusion, f32[4,512]{1,0:T(4,128)S(1)} %get-tuple-element.13, f32[4608,512,4]{1,0,2:T(8,128)} %get-tuple-element.14, pred[512,4608]{0,1:T(8,128)(4,1)S(1)} %fusion.5, bf16[4608,256]{0,1:T(8,128)(2,1)} %copy-done.13), kind=kOutput, calls=%fused_computation.17 | convolution fusion | flops 2463367168 | bytes 41828352 | tf_op jit(solution)/shard_map/kgts,skd->tkgd/dot_general | solution.py:54
  122.7 0.2 copy.22
  122.9 0.4 concatenate.48
  123.3 53.9 %all_to_all.9 = bf16[512,8,512]{2,0,1:T(8,128)(2,1)} all-to-all(bf16[512,8,512]{2,0,1:T(8,128)(2,1)S(1)} %concatenate.48), channel_id=1, replica_groups=mesh['seq'=32,'tp'=8] {'tp'}, dimensions={1} | all-to-all | bytes 8388608 | tf_op jit(solution)/shard_map/all_to_all | solution.py:12
  177.2 6.6 %copy.23 = bf16[512,8,512]{0,2,1:T(8,128)(2,1)} copy(bf16[512,8,512]{2,0,1:T(8,128)(2,1)} %all_to_all.9) | data formatting | bytes 8388608 | tf_op jit(solution)/shard_map/all_to_all | solution.py:12
  183.8 6.7 %convolution_convert_fusion = bf16[512,512]{1,0:T(8,128)(2,1)} fusion(bf16[512,4096]{0,1:T(8,128)(2,1)} %bitcast.46, bf16[4096,512]{1,0:T(8,128)(2,1)} %param.12), kind=kOutput, calls=%fused_computation.16 | convolution fusion | flops 2147745792 | bytes 8912896 | tf_op jit(solution)/shard_map/dot_general | solution.py:101
  (27 shorter events, 0.1 us)
Async XLA Ops:
  0.0 3.3 %copy-start = (bf16[4096,128]{1,0:T(8,128)(2,1)S(1)}, bf16[4096,128]{1,0:T(8,128)(2,1)}, u32[]{:S(2)}) copy-start(bf16[4096,128]{1,0:T(8,128)(2,1)} %param.11) | copy-start | bytes 3145732
  0.0 3.3 %copy-start.15 = (f32[4096]{0:T(1024)S(1)}, f32[4096]{0:T(1024)}, u32[]{:S(2)}) copy-start(f32[4096]{0:T(1024)} %param.8) | copy-start | bytes 49156
  0.0 3.8 %copy-start.2 = (bf16[512,4096]{1,0:T(8,128)(2,1)S(1)}, bf16[512,4096]{1,0:T(8,128)(2,1)}, u32[]{:S(2)}) copy-start(bf16[512,4096]{1,0:T(8,128)(2,1)} %param.7) | copy-start | bytes 12582916
  3.8 1.6 copy-start.14
  5.4 9.8 %copy-start.12 = (s32[16384]{0:T(1024)S(1)}, s32[16384]{0:T(1024)}, u32[]{:S(2)}) copy-start(s32[16384]{0:T(1024)} %param.13) | copy-start | bytes 196612
  7.0 39.7 %copy-start.16 = (f32[4096]{0:T(1024)S(1)}, f32[4096]{0:T(1024)}, u32[]{:S(2)}) copy-start(f32[4096]{0:T(1024)} %param.8) | copy-start | bytes 49156
  7.6 43.9 %copy-start.8 = (bf16[512,64]{0,1:T(8,128)(2,1)}, bf16[512,64]{0,1:T(8,128)(2,1)S(1)}, u32[]{:S(2)}) copy-start(bf16[512,64]{0,1:T(8,128)(2,1)S(1)} %get-tuple-element.9) | copy-start | bytes 196612
  7.6 43.9 %copy-start.10 = (bf16[512,64]{0,1:T(8,128)(2,1)}, bf16[512,64]{0,1:T(8,128)(2,1)S(1)}, u32[]{:S(2)}) copy-start(bf16[512,64]{0,1:T(8,128)(2,1)S(1)} %get-tuple-element.10) | copy-start | bytes 196612
  8.4 10.1 %collective-permute-start.1 = (bf16[512,256]{0,1:T(8,128)(2,1)}, bf16[512,256]{0,1:T(8,128)(2,1)S(1)}, u32[]{:S(2)}, u32[]{:S(2)}) collective-permute-start(bf16[512,256]{0,1:T(8,128)(2,1)} %pad_maximum_fusion), channel_id=1, source_target_pairs={{0,8},{8,16},{16,24},{24,32},{32,40},{40,48},{48,56},{56,64},{64,7... | collective-permute-start | bytes 786440 | tf_op jit(solution)/shard_map/ppermute | solution.py:20
  11.9 47.0 %collective-permute-start = (bf16[512,256]{0,1:T(8,128)(2,1)}, bf16[512,256]{0,1:T(8,128)(2,1)}, u32[]{:S(2)}, u32[]{:S(2)}) collective-permute-start(bf16[512,256]{0,1:T(8,128)(2,1)} %pad_maximum_fusion), channel_id=1, source_target_pairs={{0,64},{8,72},{16,80},{24,88},{32,96},{40,104},{48,112},{56,120},{... | collective-permute-start | bytes 786440 | tf_op jit(solution)/shard_map/ppermute | solution.py:20
  15.3 31.5 %copy-start.3 = (bf16[512,4096]{1,0:T(8,128)(2,1)S(1)}, bf16[512,4096]{1,0:T(8,128)(2,1)}, u32[]{:S(2)}) copy-start(bf16[512,4096]{1,0:T(8,128)(2,1)} %param.7) | copy-start | bytes 12582916
  18.5 33.0 %copy-start.4 = (bf16[512,256]{0,1:T(8,128)(2,1)}, bf16[512,256]{0,1:T(8,128)(2,1)S(1)}, u32[]{:S(2)}) copy-start(bf16[512,256]{0,1:T(8,128)(2,1)S(1)} %collective-permute-done.1) | copy-start | bytes 786436
  18.6 25.1 %collective-permute-start.2 = (bf16[1024,256]{0,1:T(8,128)(2,1)S(1)}, bf16[1024,256]{0,1:T(8,128)(2,1)S(1)}, u32[]{:S(2)}, u32[]{:S(2)}) collective-permute-start(bf16[1024,256]{0,1:T(8,128)(2,1)S(1)} %maximum_maximum_fusion.1), channel_id=1, source_target_pairs={{0,16},{8,24},{16,32},{24,40},{32,48},{40,56},{48,64},{56,72},{64,... | collective-permute-start | bytes 1572872 | tf_op jit(solution)/shard_map/ppermute | solution.py:20
  43.6 7.9 %copy-start.6 = (bf16[1024,256]{0,1:T(8,128)(2,1)}, bf16[1024,256]{0,1:T(8,128)(2,1)S(1)}, u32[]{:S(2)}) copy-start(bf16[1024,256]{0,1:T(8,128)(2,1)S(1)} %collective-permute-done.2) | copy-start | bytes 1572868
  44.8 27.5 %collective-permute-start.3 = (bf16[2048,256]{0,1:T(8,128)(2,1)}, bf16[2048,256]{0,1:T(8,128)(2,1)}, u32[]{:S(2)}, u32[]{:S(2)}) collective-permute-start(bf16[2048,256]{0,1:T(8,128)(2,1)} %maximum_maximum_fusion), channel_id=1, source_target_pairs={{0,32},{8,40},{16,48},{24,56},{32,64},{40,72},{48,80},{56,88},{64,... | collective-permute-start | bytes 3145736 | tf_op jit(solution)/shard_map/ppermute | solution.py:20
  56.4 17.2 %copy-start.7 = (bf16[1024,256]{0,1:T(8,128)(2,1)S(1)}, bf16[1024,256]{0,1:T(8,128)(2,1)}, u32[]{:S(2)}) copy-start(bf16[1024,256]{0,1:T(8,128)(2,1)} %copy-done.6) | copy-start | bytes 1572868
  56.4 17.3 %copy-start.5 = (bf16[512,256]{0,1:T(8,128)(2,1)S(1)}, bf16[512,256]{0,1:T(8,128)(2,1)}, u32[]{:S(2)}) copy-start(bf16[512,256]{0,1:T(8,128)(2,1)} %copy-done.4) | copy-start | bytes 786436
  56.4 17.3 %copy-start.9 = (bf16[512,64]{0,1:T(8,128)(2,1)S(1)}, bf16[512,64]{0,1:T(8,128)(2,1)}, u32[]{:S(2)}) copy-start(bf16[512,64]{0,1:T(8,128)(2,1)} %copy-done.8) | copy-start | bytes 196612
  56.4 17.3 %copy-start.11 = (bf16[512,64]{0,1:T(8,128)(2,1)S(1)}, bf16[512,64]{0,1:T(8,128)(2,1)}, u32[]{:S(2)}) copy-start(bf16[512,64]{0,1:T(8,128)(2,1)} %copy-done.10) | copy-start | bytes 196612
  73.7 15.4 %copy-start.13 = (bf16[4608,256]{0,1:T(8,128)(2,1)}, bf16[4608,256]{0,1:T(8,128)(2,1)S(1)}, u32[]{:S(2)}) copy-start(bf16[4608,256]{0,1:T(8,128)(2,1)S(1)} %constant_dynamic-update-slice_fusion) | copy-start | bytes 7077892
  183.8 6.7 %copy-start.1 = (bf16[4096,128]{1,0:T(8,128)(2,1)S(1)}, bf16[4096,128]{1,0:T(8,128)(2,1)}, u32[]{:S(2)}) copy-start(bf16[4096,128]{1,0:T(8,128)(2,1)} %param.11) | copy-start | bytes 3145732
